TPU v7x, 512 devices: a whole 4x4x16 slice. The times are simulated.
512 devices in a mesh: slab: 64 (over z, x), sec: 8 (over y, core).
Axes of the slice: x: 4, y: 4, z: 16, core: 2. Of those that a mesh axis runs over, the one named last changes fastest.
Arguments:
- source: float32 [64, 65536], P(None, ('slab', 'sec'))
- fine_blocks: bfloat16 [3, 64, 64, 65536], P(None, None, None, ('slab', 'sec'))
- fine_pattern: int32 [3, 65536], P(None, ('slab', 'sec')), may hold values from 0 to 65535, as said below
- fine_prolong: bfloat16 [3, 64, 6, 65536], P(None, None, None, ('slab', 'sec')), may hold values from -0.75 to 0.75
- prolong_pattern: int32 [3, 65536], P(None, ('slab', 'sec')), may hold values from 0 to 65535, as said below
- coarse_blocks: bfloat16 [3, 6, 6, 65536], P(None, None, None, 'slab')
- coarse_pattern: int32 [3, 65536], P(None, 'slab'), may hold values from 0 to 65535, as said below
- section_prolong: bfloat16 [3, 6, 24, 65536], P(None, None, None, 'slab'), may hold values from -0.046875 to 0.046875
- coarsest_inverse: float32 [1536, 1536], P('slab')
Outputs:
- solution: float32 [64, 65536], P(None, ('slab', 'sec'))
Inputs may be any that keep to these rules, and one draw needn't show every extreme that they name: `fine_pattern`: row 0 names the aggregate itself; the other rows name aggregates at most 96 away, and distance exactly 96 occurs in every draw. `prolong_pattern`: row 0 names the aggregate's own coarse block; the other rows name coarse blocks at most 96 away, and distance exactly 96 occurs in every draw. `coarse_pattern`: row 0 names the block itself; the other rows name coarse blocks at most 96 away, and distance exactly 96 occurs in every draw.
All inputs are finite; a program needn't handle non-finite values.
Results may differ from a plain program's by a relative error of at most 0.0003.
Values sent between devices are 32-bit elements; how exact they have to be, the bound alone decides.
No kernel may reach another device: no remote copies, remote signals or barrier semaphores. Data moves between devices by JAX's collectives and lax.ppermute only.
A program may use at most 64 MiB of HBM per device.

v0:
```python
import jax
import jax.numpy as jnp
from jax import lax
from jax.sharding import PartitionSpec as P

HB = 96
CYCLES = 2
KEEP = 1.0 / 7.0
FRESH = 8.0 / 7.0


def padded(array, sides, width):
    for axis, dim in sides:
        count, length = (lax.axis_size(axis), array.shape[dim])
        up = [(i, (i + 1) % count) for i in range(count - 1)]
        down = [(j, i) for i, j in up]
        last = lax.slice_in_dim(array, length - width, length, axis=dim)
        leading = lax.slice_in_dim(array, 0, width, axis=dim)
        before = lax.ppermute(last, axis, up)
        after = lax.ppermute(leading, axis, down)
        array = jnp.concatenate([before, array, after], axis=dim)
    return array


def from_behind(value, axis, steps):
    count = lax.axis_size(axis)
    leading, last = (max(0, -steps), min(count, count - steps))
    return lax.ppermute(value, axis, [(source, source + steps) for source in range(leading, last)])


def inverse_diagonal(matrix):
    return 1.0 / jnp.diagonal(matrix[0], axis1=0, axis2=1).T.astype(jnp.float32)


def apply_local(matrix, local_cols, extended):
    picked = jnp.swapaxes(extended[:, local_cols], 0, 1)
    return jnp.sum(matrix * picked[:, None, :, :], axis=(0, 2))


def smooth(operator, inverse, rhs, start):
    if start is None:
        change = inverse * rhs
        field = change
    else:
        change = inverse * (rhs - operator(start))
        field = start + change
    change = KEEP * change + FRESH * inverse * (rhs - operator(field))
    return field + change


def shards(
    source,
    fine_blocks,
    fine_pattern,
    fine_prolong,
    prolong_pattern,
    coarse_blocks,
    coarse_pattern,
    section_prolong,
    coarsest_inverse,
):
    reach = HB
    own_rows = source.shape[1]
    section_rows = coarse_blocks.shape[3]
    device = lax.axis_index(("slab", "sec"))
    section = lax.axis_index("slab")
    fine_cols = fine_pattern - (device * own_rows - reach)
    coarse_cols = coarse_pattern - (section * section_rows - reach)
    gather_cols = prolong_pattern - (section * section_rows - reach)
    fine_inverse = inverse_diagonal(fine_blocks)
    coarse_inverse = inverse_diagonal(coarse_blocks)

    def fine_apply(field):
        extended = padded(field, ((("slab", "sec"), 1),), reach)
        return apply_local(fine_blocks, fine_cols, extended)

    def coarse_extend(field):
        return padded(field, (("slab", 1),), reach)

    def coarse_apply(field):
        return apply_local(coarse_blocks, coarse_cols, coarse_extend(field))

    solution = None
    for turn_index in range(CYCLES):
        solution = smooth(fine_apply, fine_inverse, source, solution)
        residual = source - fine_apply(solution)
        terms = jnp.sum(fine_prolong * residual[None, :, None, :], axis=1)
        modes = terms.shape[1]
        flat = jnp.swapaxes(terms, 0, 1).reshape(modes, -1)
        slots = gather_cols.reshape(-1)
        partial_sum = (
            jnp.zeros((modes, section_rows + 2 * reach), jnp.float32).at[:, slots].add(flat)
        )
        partial_sum = lax.psum(partial_sum, "sec")
        lower = from_behind(partial_sum[:, section_rows + reach :], "slab", 1)
        upper = from_behind(partial_sum[:, :reach], "slab", -1)
        inner = partial_sum[:, reach : reach + section_rows]
        coarse_rhs = inner.at[:, :reach].add(lower).at[:, section_rows - reach :].add(upper)
        coarse_sol = smooth(coarse_apply, coarse_inverse, coarse_rhs, None)
        coarse_res = coarse_rhs - coarse_apply(coarse_sol)
        parts = jnp.sum(section_prolong * coarse_res[None, :, None, :], axis=(1, 3))
        width = parts.shape[1]
        every = lax.all_gather(parts[None], "slab", axis=0, tiled=True)
        zero = jnp.zeros((1, width), jnp.float32)
        total = (
            every[:, 1]
            + jnp.concatenate([every[1:, 0], zero], 0)
            + jnp.concatenate([zero, every[:-1, 2]], 0)
        )
        answer = jnp.dot(coarsest_inverse, total.reshape(-1), precision=lax.Precision.HIGHEST)
        nearby = padded(answer[None, :], (("slab", 0),), 1)
        coarse_sol = coarse_sol + jnp.sum(section_prolong * nearby[:, None, :, None], axis=(0, 2))
        coarse_sol = smooth(coarse_apply, coarse_inverse, coarse_rhs, coarse_sol)
        prolong_extended = coarse_extend(coarse_sol)
        picked = jnp.swapaxes(prolong_extended[:, gather_cols], 0, 1)
        solution = solution + jnp.sum(fine_prolong * picked[:, None, :, :], axis=(0, 2))
        solution = smooth(fine_apply, fine_inverse, source, solution)
    return solution


def solution(mesh):
    in_specs = (
        P(None, ("slab", "sec")),
        P(None, None, None, ("slab", "sec")),
        P(None, ("slab", "sec")),
        P(None, None, None, ("slab", "sec")),
        P(None, ("slab", "sec")),
        P(None, None, None, "slab"),
        P(None, "slab"),
        P(None, None, None, "slab"),
        P("slab", None),
    )
    out_specs = P(None, ("slab", "sec"))
    return jax.shard_map(shards, mesh=mesh, in_specs=in_specs, out_specs=out_specs, check_vma=False)
```

profile of v0, /device:TPU:127, one launch (start us, length us, event | category | flops | bytes accessed | tf_op | source)
XLA Modules:
  0.0 759.0 jit_solution(1430777949323937785)
XLA Ops:
  4.9 4.9 collective-permute-start
  25.9 5.1 collective-permute-start.2
  33.6 8.1 %collective-permute-done.3 = f32[64,96]{1,0:T(8,128)S(1)} collective-permute-done((f32[64,96]{1,0:T(8,128)S(1)}, f32[64,96]{1,0:T(8,128)S(1)}, u32[]{:S(2)}, u32[]{:S(2)}) %collective-permute-start.3) | collective-permute-done | bytes 24608 | tf_op jit(solution)/shard_map/ppermute | solution.py:20
  53.9 23.9 %psum.14 = f32[6,1216]{1,0:T(8,128)S(1)} all-reduce(f32[6,1216]{1,0:T(8,128)S(1)} %copy.153), channel_id=1, replica_groups=mesh['slab'=64,'sec'=8] {'sec'}, use_global_device_ids=true, to_apply=%region_4.5 | all-reduce | flops 7296 | bytes 58368 | tf_op jit(solution)/shard_map/psum | solution.py:94
  100.5 11.9 %gather_fusion.4 = f32[3072,6]{1,0:T(8,128)} fusion(f32[6,1216]{0,1:T(8,128)} %copy.154, s32[3072]{0:T(1024)S(1)} %broadcast_clamp_fusion), kind=kCustom, calls=%fused_computation.4 | custom fusion | bytes 159744 | tf_op jit(solution)/shard_map/gather | solution.py:36
  120.8 4.3 collective-permute-done.9
  126.3 11.9 %gather_fusion.5 = f32[3072,6]{1,0:T(8,128)} fusion(f32[6,1216]{0,1:T(8,128)} %copy.156, s32[3072]{0:T(1024)S(1)} %broadcast_clamp_fusion), kind=kCustom, calls=%fused_computation.5 | custom fusion | bytes 159744 | tf_op jit(solution)/shard_map/gather | solution.py:36
  142.6 72.8 %all-gather.2 = f32[64,3,24]{2,1,0:T(4,128)S(1)} all-gather(f32[1,3,24]{2,1,0:T(4,128)S(1)} %bitcast.134), channel_id=2, replica_groups=mesh['slab'=64,'sec'=8] {'slab'}, dimensions={0}, use_global_device_ids=true | all-gather | bytes 18720 | tf_op jit(solution)/shard_map/all_gather | solution.py:103
  222.4 5.7 collective-permute-done.11
  234.9 4.3 collective-permute-done.13
  240.4 11.9 %gather_fusion.6 = f32[3072,6]{1,0:T(8,128)} fusion(f32[6,1216]{0,1:T(8,128)} %copy.162, s32[3072]{0:T(1024)S(1)} %broadcast_clamp_fusion), kind=kCustom, calls=%fused_computation.6 | custom fusion | bytes 159744 | tf_op jit(solution)/shard_map/gather | solution.py:36
  261.3 4.3 collective-permute-done.15
  268.2 11.9 %gather_fusion.7 = f32[3072,6]{1,0:T(8,128)} fusion(f32[6,1216]{0,1:T(8,128)} %copy.164, s32[3072]{0:T(1024)S(1)} %broadcast_clamp_fusion), kind=kCustom, calls=%fused_computation.7 | custom fusion | bytes 159744 | tf_op jit(solution)/shard_map/gather | solution.py:36
  299.4 38.0 %collective-permute-start.18 = (f32[64,96]{1,0:T(8,128)S(1)}, f32[64,96]{1,0:T(8,128)S(1)}, u32[]{:S(2)}, u32[]{:S(2)}) collective-permute-start(f32[64,96]{1,0:T(8,128)S(1)} %get-tuple-element.83), channel_id=1, source_target_pairs={{0,1},{1,2},{2,3},{3,4},{4,5},{5,6},{6,7},{7,8},{8,9},{9,10},{10,1... | collective-permute-start | bytes 73736 | tf_op jit(solution)/shard_map/ppermute | solution.py:19
  339.5 8.5 %collective-permute-done.19 = f32[64,96]{1,0:T(8,128)S(1)} collective-permute-done((f32[64,96]{1,0:T(8,128)S(1)}, f32[64,96]{1,0:T(8,128)S(1)}, u32[]{:S(2)}, u32[]{:S(2)}) %collective-permute-start.19) | collective-permute-done | bytes 24608 | tf_op jit(solution)/shard_map/ppermute | solution.py:20
  357.8 8.2 %collective-permute-done.21 = f32[64,96]{1,0:T(8,128)S(1)} collective-permute-done((f32[64,96]{1,0:T(8,128)S(1)}, f32[64,96]{1,0:T(8,128)S(1)}, u32[]{:S(2)}, u32[]{:S(2)}) %collective-permute-start.21) | collective-permute-done | bytes 24608 | tf_op jit(solution)/shard_map/ppermute | solution.py:20
  375.7 8.2 %collective-permute-done.23 = f32[64,96]{1,0:T(8,128)S(1)} collective-permute-done((f32[64,96]{1,0:T(8,128)S(1)}, f32[64,96]{1,0:T(8,128)S(1)}, u32[]{:S(2)}, u32[]{:S(2)}) %collective-permute-start.23) | collective-permute-done | bytes 24608 | tf_op jit(solution)/shard_map/ppermute | solution.py:20
  396.7 8.2 %collective-permute-done.25 = f32[64,96]{1,0:T(8,128)S(1)} collective-permute-done((f32[64,96]{1,0:T(8,128)S(1)}, f32[64,96]{1,0:T(8,128)S(1)}, u32[]{:S(2)}, u32[]{:S(2)}) %collective-permute-start.25) | collective-permute-done | bytes 24608 | tf_op jit(solution)/shard_map/ppermute | solution.py:20
  417.7 8.2 %collective-permute-done.27 = f32[64,96]{1,0:T(8,128)S(1)} collective-permute-done((f32[64,96]{1,0:T(8,128)S(1)}, f32[64,96]{1,0:T(8,128)S(1)}, u32[]{:S(2)}, u32[]{:S(2)}) %collective-permute-start.27) | collective-permute-done | bytes 24608 | tf_op jit(solution)/shard_map/ppermute | solution.py:20
  440.1 24.5 %psum.15 = f32[6,1216]{1,0:T(8,128)S(1)} all-reduce(f32[6,1216]{1,0:T(8,128)} %copy.179), channel_id=1, replica_groups=mesh['slab'=64,'sec'=8] {'sec'}, use_global_device_ids=true, to_apply=%region_20.21 | all-reduce | flops 7296 | bytes 58368 | tf_op jit(solution)/shard_map/psum | solution.py:94
  479.9 4.3 collective-permute-done.31
  485.4 11.9 %gather_fusion.14 = f32[3072,6]{1,0:T(8,128)} fusion(f32[6,1216]{0,1:T(8,128)} %copy.180, s32[3072]{0:T(1024)S(1)} %broadcast_clamp_fusion), kind=kCustom, calls=%fused_computation.14 | custom fusion | bytes 159744 | tf_op jit(solution)/shard_map/gather | solution.py:36
  511.8 11.9 %gather_fusion.15 = f32[3072,6]{1,0:T(8,128)} fusion(f32[6,1216]{0,1:T(8,128)} %copy.182, s32[3072]{0:T(1024)S(1)} %broadcast_clamp_fusion), kind=kCustom, calls=%fused_computation.15 | custom fusion | bytes 159744 | tf_op jit(solution)/shard_map/gather | solution.py:36
  528.8 70.7 %all-gather.3 = f32[64,3,24]{2,1,0:T(4,128)S(1)} all-gather(f32[1,3,24]{2,1,0:T(4,128)S(1)} %bitcast.135), channel_id=3, replica_groups=mesh['slab'=64,'sec'=8] {'slab'}, dimensions={0}, use_global_device_ids=true | all-gather | bytes 18720 | tf_op jit(solution)/shard_map/all_gather | solution.py:103
  609.6 5.7 collective-permute-done.35
  627.6 11.9 %gather_fusion.16 = f32[3072,6]{1,0:T(8,128)} fusion(f32[6,1216]{0,1:T(8,128)} %copy.188, s32[3072]{0:T(1024)S(1)} %broadcast_clamp_fusion), kind=kCustom, calls=%fused_computation.16 | custom fusion | bytes 159744 | tf_op jit(solution)/shard_map/gather | solution.py:36
  648.5 4.3 collective-permute-done.39
  655.3 11.9 %gather_fusion.17 = f32[3072,6]{1,0:T(8,128)} fusion(f32[6,1216]{0,1:T(8,128)} %copy.190, s32[3072]{0:T(1024)S(1)} %broadcast_clamp_fusion), kind=kCustom, calls=%fused_computation.17 | custom fusion | bytes 159744 | tf_op jit(solution)/shard_map/gather | solution.py:36
  676.2 4.3 collective-permute-done.41
  686.5 38.0 %collective-permute-start.42 = (f32[64,96]{1,0:T(8,128)S(1)}, f32[64,96]{1,0:T(8,128)S(1)}, u32[]{:S(2)}, u32[]{:S(2)}) collective-permute-start(f32[64,96]{1,0:T(8,128)S(1)} %get-tuple-element.63), channel_id=1, source_target_pairs={{0,1},{1,2},{2,3},{3,4},{4,5},{5,6},{6,7},{7,8},{8,9},{9,10},{10,1... | collective-permute-start | bytes 73736 | tf_op jit(solution)/shard_map/ppermute | solution.py:19
  726.5 8.7 %collective-permute-done.43 = f32[64,96]{1,0:T(8,128)S(1)} collective-permute-done((f32[64,96]{1,0:T(8,128)S(1)}, f32[64,96]{1,0:T(8,128)S(1)}, u32[]{:S(2)}, u32[]{:S(2)}) %collective-permute-start.43) | collective-permute-done | bytes 24608 | tf_op jit(solution)/shard_map/ppermute | solution.py:20
  744.9 8.2 %collective-permute-done.45 = f32[64,96]{1,0:T(8,128)S(1)} collective-permute-done((f32[64,96]{1,0:T(8,128)S(1)}, f32[64,96]{1,0:T(8,128)S(1)}, u32[]{:S(2)}, u32[]{:S(2)}) %collective-permute-start.45) | collective-permute-done | bytes 24608 | tf_op jit(solution)/shard_map/ppermute | solution.py:20
  (295 shorter events, 281.2 us)
Async XLA Ops:
  4.9 11.6 %collective-permute-start = (f32[64,96]{1,0:T(8,128)S(1)}, f32[64,96]{1,0:T(8,128)S(1)}, u32[]{:S(2)}, u32[]{:S(2)}) collective-permute-start(f32[64,96]{1,0:T(8,128)S(1)} %get-tuple-element.97), channel_id=1, source_target_pairs={{0,1},{1,2},{2,3},{3,4},{4,5},{5,6},{6,7},{7,8},{8,9},{9,10},{10,1... | collective-permute-start | bytes 73736 | tf_op jit(solution)/shard_map/ppermute | solution.py:19
  9.8 10.7 %collective-permute-start.1 = (f32[64,96]{1,0:T(8,128)S(1)}, f32[64,96]{1,0:T(8,128)S(1)}, u32[]{:S(2)}, u32[]{:S(2)}) collective-permute-start(f32[64,96]{1,0:T(8,128)S(1)} %get-tuple-element.98), channel_id=1, source_target_pairs={{1,0},{2,1},{3,2},{4,3},{5,4},{6,5},{7,6},{8,7},{9,8},{10,9},{11,1... | collective-permute-start | bytes 73736 | tf_op jit(solution)/shard_map/ppermute | solution.py:20
  25.9 7.7 %collective-permute-start.2 = (f32[64,96]{1,0:T(8,128)S(1)}, f32[64,96]{1,0:T(8,128)S(1)}, u32[]{:S(2)}, u32[]{:S(2)}) collective-permute-start(f32[64,96]{1,0:T(8,128)S(1)} %get-tuple-element.95), channel_id=1, source_target_pairs={{0,1},{1,2},{2,3},{3,4},{4,5},{5,6},{6,7},{7,8},{8,9},{9,10},{10,1... | collective-permute-start | bytes 73736 | tf_op jit(solution)/shard_map/ppermute | solution.py:19
  31.1 10.7 %collective-permute-start.3 = (f32[64,96]{1,0:T(8,128)S(1)}, f32[64,96]{1,0:T(8,128)S(1)}, u32[]{:S(2)}, u32[]{:S(2)}) collective-permute-start(f32[64,96]{1,0:T(8,128)S(1)} %get-tuple-element.96), channel_id=1, source_target_pairs={{1,0},{2,1},{3,2},{4,3},{5,4},{6,5},{7,6},{8,7},{9,8},{10,9},{11,1... | collective-permute-start | bytes 73736 | tf_op jit(solution)/shard_map/ppermute | solution.py:20
  77.8 7.3 collective-permute-start.4
  81.8 7.7 %collective-permute-start.5 = (f32[6,96]{1,0:T(8,128)S(1)}, f32[6,96]{1,0:T(8,128)S(1)}, u32[]{:S(2)}, u32[]{:S(2)}) collective-permute-start(f32[6,96]{1,0:T(8,128)S(1)} %get-tuple-element.59), channel_id=1, source_target_pairs={{8,0},{16,8},{24,16},{32,24},{40,32},{48,40},{56,48},{64,56},{72,6... | collective-permute-start | bytes 6920 | tf_op jit(solution)/shard_map/ppermute | solution.py:28
  89.8 6.0 collective-permute-start.6
  91.7 7.7 %collective-permute-start.7 = (f32[6,96]{1,0:T(8,128)S(1)}, f32[6,96]{1,0:T(8,128)S(1)}, u32[]{:S(2)}, u32[]{:S(2)}) collective-permute-start(f32[6,96]{1,0:T(8,128)S(1)} %get-tuple-element.93), channel_id=1, source_target_pairs={{8,0},{16,8},{24,16},{32,24},{40,32},{48,40},{56,48},{64,56},{72,6... | collective-permute-start | bytes 6920 | tf_op jit(solution)/shard_map/ppermute | solution.py:20
  117.4 7.7 %collective-permute-start.9 = (f32[6,96]{1,0:T(8,128)S(1)}, f32[6,96]{1,0:T(8,128)S(1)}, u32[]{:S(2)}, u32[]{:S(2)}) collective-permute-start(f32[6,96]{1,0:T(8,128)S(1)} %get-tuple-element.91), channel_id=1, source_target_pairs={{8,0},{16,8},{24,16},{32,24},{40,32},{48,40},{56,48},{64,56},{72,6... | collective-permute-start | bytes 6920 | tf_op jit(solution)/shard_map/ppermute | solution.py:20
  216.3 6.1 collective-permute-start.10
  220.5 7.6 %collective-permute-start.11 = (f32[1,24]{1,0:T(1,128)S(1)}, f32[1,24]{1,0:T(1,128)S(1)}, u32[]{:S(2)}, u32[]{:S(2)}) collective-permute-start(f32[1,24]{1,0:T(1,128)S(1)} %fusion.65), channel_id=1, source_target_pairs={{8,0},{16,8},{24,16},{32,24},{40,32},{48,40},{56,48},{64,56},{72,6... | collective-permute-start | bytes 296 | tf_op jit(solution)/shard_map/ppermute | solution.py:20
  231.5 7.7 %collective-permute-start.13 = (f32[6,96]{1,0:T(8,128)S(1)}, f32[6,96]{1,0:T(8,128)S(1)}, u32[]{:S(2)}, u32[]{:S(2)}) collective-permute-start(f32[6,96]{1,0:T(8,128)S(1)} %get-tuple-element.89), channel_id=1, source_target_pairs={{8,0},{16,8},{24,16},{32,24},{40,32},{48,40},{56,48},{64,56},{72,6... | collective-permute-start | bytes 6920 | tf_op jit(solution)/shard_map/ppermute | solution.py:20
  257.9 7.7 %collective-permute-start.15 = (f32[6,96]{1,0:T(8,128)S(1)}, f32[6,96]{1,0:T(8,128)S(1)}, u32[]{:S(2)}, u32[]{:S(2)}) collective-permute-start(f32[6,96]{1,0:T(8,128)S(1)} %get-tuple-element.87), channel_id=1, source_target_pairs={{8,0},{16,8},{24,16},{32,24},{40,32},{48,40},{56,48},{64,56},{72,6... | collective-permute-start | bytes 6920 | tf_op jit(solution)/shard_map/ppermute | solution.py:20
  285.7 7.7 %collective-permute-start.17 = (f32[6,96]{1,0:T(8,128)S(1)}, f32[6,96]{1,0:T(8,128)S(1)}, u32[]{:S(2)}, u32[]{:S(2)}) collective-permute-start(f32[6,96]{1,0:T(8,128)S(1)} %get-tuple-element.85), channel_id=1, source_target_pairs={{8,0},{16,8},{24,16},{32,24},{40,32},{48,40},{56,48},{64,56},{72,6... | collective-permute-start | bytes 6920 | tf_op jit(solution)/shard_map/ppermute | solution.py:20
  299.4 40.1 %collective-permute-start.18 = (f32[64,96]{1,0:T(8,128)S(1)}, f32[64,96]{1,0:T(8,128)S(1)}, u32[]{:S(2)}, u32[]{:S(2)}) collective-permute-start(f32[64,96]{1,0:T(8,128)S(1)} %get-tuple-element.83), channel_id=1, source_target_pairs={{0,1},{1,2},{2,3},{3,4},{4,5},{5,6},{6,7},{7,8},{8,9},{9,10},{10,1... | collective-permute-start | bytes 73736 | tf_op jit(solution)/shard_map/ppermute | solution.py:19
  337.4 10.7 %collective-permute-start.19 = (f32[64,96]{1,0:T(8,128)S(1)}, f32[64,96]{1,0:T(8,128)S(1)}, u32[]{:S(2)}, u32[]{:S(2)}) collective-permute-start(f32[64,96]{1,0:T(8,128)S(1)} %get-tuple-element.84), channel_id=1, source_target_pairs={{1,0},{2,1},{3,2},{4,3},{5,4},{6,5},{7,6},{8,7},{9,8},{10,9},{11,1... | collective-permute-start | bytes 73736 | tf_op jit(solution)/shard_map/ppermute | solution.py:20
  355.4 10.7 %collective-permute-start.21 = (f32[64,96]{1,0:T(8,128)S(1)}, f32[64,96]{1,0:T(8,128)S(1)}, u32[]{:S(2)}, u32[]{:S(2)}) collective-permute-start(f32[64,96]{1,0:T(8,128)S(1)} %get-tuple-element.82), channel_id=1, source_target_pairs={{1,0},{2,1},{3,2},{4,3},{5,4},{6,5},{7,6},{8,7},{9,8},{10,9},{11,1... | collective-permute-start | bytes 73736 | tf_op jit(solution)/shard_map/ppermute | solution.py:20
  373.3 10.7 %collective-permute-start.23 = (f32[64,96]{1,0:T(8,128)S(1)}, f32[64,96]{1,0:T(8,128)S(1)}, u32[]{:S(2)}, u32[]{:S(2)}) collective-permute-start(f32[64,96]{1,0:T(8,128)S(1)} %get-tuple-element.80), channel_id=1, source_target_pairs={{1,0},{2,1},{3,2},{4,3},{5,4},{6,5},{7,6},{8,7},{9,8},{10,9},{11,1... | collective-permute-start | bytes 73736 | tf_op jit(solution)/shard_map/ppermute | solution.py:20
  394.3 10.7 %collective-permute-start.25 = (f32[64,96]{1,0:T(8,128)S(1)}, f32[64,96]{1,0:T(8,128)S(1)}, u32[]{:S(2)}, u32[]{:S(2)}) collective-permute-start(f32[64,96]{1,0:T(8,128)S(1)} %get-tuple-element.78), channel_id=1, source_target_pairs={{1,0},{2,1},{3,2},{4,3},{5,4},{6,5},{7,6},{8,7},{9,8},{10,9},{11,1... | collective-permute-start | bytes 73736 | tf_op jit(solution)/shard_map/ppermute | solution.py:20
  415.3 10.7 %collective-permute-start.27 = (f32[64,96]{1,0:T(8,128)S(1)}, f32[64,96]{1,0:T(8,128)S(1)}, u32[]{:S(2)}, u32[]{:S(2)}) collective-permute-start(f32[64,96]{1,0:T(8,128)S(1)} %get-tuple-element.76), channel_id=1, source_target_pairs={{1,0},{2,1},{3,2},{4,3},{5,4},{6,5},{7,6},{8,7},{9,8},{10,9},{11,1... | collective-permute-start | bytes 73736 | tf_op jit(solution)/shard_map/ppermute | solution.py:20
  464.7 5.4 collective-permute-start.28
  466.6 7.7 %collective-permute-start.29 = (f32[6,96]{1,0:T(8,128)S(1)}, f32[6,96]{1,0:T(8,128)S(1)}, u32[]{:S(2)}, u32[]{:S(2)}) collective-permute-start(f32[6,96]{1,0:T(8,128)S(1)} %get-tuple-element.57), channel_id=1, source_target_pairs={{8,0},{16,8},{24,16},{32,24},{40,32},{48,40},{56,48},{64,56},{72,6... | collective-permute-start | bytes 6920 | tf_op jit(solution)/shard_map/ppermute | solution.py:28
  476.6 7.7 %collective-permute-start.31 = (f32[6,96]{1,0:T(8,128)S(1)}, f32[6,96]{1,0:T(8,128)S(1)}, u32[]{:S(2)}, u32[]{:S(2)}) collective-permute-start(f32[6,96]{1,0:T(8,128)S(1)} %get-tuple-element.73), channel_id=1, source_target_pairs={{8,0},{16,8},{24,16},{32,24},{40,32},{48,40},{56,48},{64,56},{72,6... | collective-permute-start | bytes 6920 | tf_op jit(solution)/shard_map/ppermute | solution.py:20
  502.9 7.7 %collective-permute-start.33 = (f32[6,96]{1,0:T(8,128)S(1)}, f32[6,96]{1,0:T(8,128)S(1)}, u32[]{:S(2)}, u32[]{:S(2)}) collective-permute-start(f32[6,96]{1,0:T(8,128)S(1)} %get-tuple-element.71), channel_id=1, source_target_pairs={{8,0},{16,8},{24,16},{32,24},{40,32},{48,40},{56,48},{64,56},{72,6... | collective-permute-start | bytes 6920 | tf_op jit(solution)/shard_map/ppermute | solution.py:20
  603.5 6.1 collective-permute-start.34
  607.7 7.6 %collective-permute-start.35 = (f32[1,24]{1,0:T(1,128)S(1)}, f32[1,24]{1,0:T(1,128)S(1)}, u32[]{:S(2)}, u32[]{:S(2)}) collective-permute-start(f32[1,24]{1,0:T(1,128)S(1)} %fusion.66), channel_id=1, source_target_pairs={{8,0},{16,8},{24,16},{32,24},{40,32},{48,40},{56,48},{64,56},{72,6... | collective-permute-start | bytes 296 | tf_op jit(solution)/shard_map/ppermute | solution.py:20
  618.7 7.7 %collective-permute-start.37 = (f32[6,96]{1,0:T(8,128)S(1)}, f32[6,96]{1,0:T(8,128)S(1)}, u32[]{:S(2)}, u32[]{:S(2)}) collective-permute-start(f32[6,96]{1,0:T(8,128)S(1)} %get-tuple-element.69), channel_id=1, source_target_pairs={{8,0},{16,8},{24,16},{32,24},{40,32},{48,40},{56,48},{64,56},{72,6... | collective-permute-start | bytes 6920 | tf_op jit(solution)/shard_map/ppermute | solution.py:20
  645.1 7.7 %collective-permute-start.39 = (f32[6,96]{1,0:T(8,128)S(1)}, f32[6,96]{1,0:T(8,128)S(1)}, u32[]{:S(2)}, u32[]{:S(2)}) collective-permute-start(f32[6,96]{1,0:T(8,128)S(1)} %get-tuple-element.67), channel_id=1, source_target_pairs={{8,0},{16,8},{24,16},{32,24},{40,32},{48,40},{56,48},{64,56},{72,6... | collective-permute-start | bytes 6920 | tf_op jit(solution)/shard_map/ppermute | solution.py:20
  672.9 7.7 %collective-permute-start.41 = (f32[6,96]{1,0:T(8,128)S(1)}, f32[6,96]{1,0:T(8,128)S(1)}, u32[]{:S(2)}, u32[]{:S(2)}) collective-permute-start(f32[6,96]{1,0:T(8,128)S(1)} %get-tuple-element.65), channel_id=1, source_target_pairs={{8,0},{16,8},{24,16},{32,24},{40,32},{48,40},{56,48},{64,56},{72,6... | collective-permute-start | bytes 6920 | tf_op jit(solution)/shard_map/ppermute | solution.py:20
  686.5 40.0 %collective-permute-start.42 = (f32[64,96]{1,0:T(8,128)S(1)}, f32[64,96]{1,0:T(8,128)S(1)}, u32[]{:S(2)}, u32[]{:S(2)}) collective-permute-start(f32[64,96]{1,0:T(8,128)S(1)} %get-tuple-element.63), channel_id=1, source_target_pairs={{0,1},{1,2},{2,3},{3,4},{4,5},{5,6},{6,7},{7,8},{8,9},{9,10},{10,1... | collective-permute-start | bytes 73736 | tf_op jit(solution)/shard_map/ppermute | solution.py:19
  724.6 10.7 %collective-permute-start.43 = (f32[64,96]{1,0:T(8,128)S(1)}, f32[64,96]{1,0:T(8,128)S(1)}, u32[]{:S(2)}, u32[]{:S(2)}) collective-permute-start(f32[64,96]{1,0:T(8,128)S(1)} %get-tuple-element.64), channel_id=1, source_target_pairs={{1,0},{2,1},{3,2},{4,3},{5,4},{6,5},{7,6},{8,7},{9,8},{10,9},{11,1... | collective-permute-start | bytes 73736 | tf_op jit(solution)/shard_map/ppermute | solution.py:20
  742.5 10.7 %collective-permute-start.45 = (f32[64,96]{1,0:T(8,128)S(1)}, f32[64,96]{1,0:T(8,128)S(1)}, u32[]{:S(2)}, u32[]{:S(2)}) collective-permute-start(f32[64,96]{1,0:T(8,128)S(1)} %get-tuple-element.62), channel_id=1, source_target_pairs={{1,0},{2,1},{3,2},{4,3},{5,4},{6,5},{7,6},{8,7},{9,8},{10,9},{11,1... | collective-permute-start | bytes 73736 | tf_op jit(solution)/shard_map/ppermute | solution.py:20
  (31 other events, 636.0 us)
where the time goes:
time: 763 us; the launch traced here: 759 us
  local copies, waits for them, and re-layouts  195 us (26%)
  blocking collectives  192 us (25%)
  starting transfers between devices  191 us (25%)
  waiting for transfers between devices  131 us (17%)
  other arithmetic  49.2 us (6%)
    all_gather x2, blocking collectives, shards(): every = lax.all_gather(parts[None], 'slab', axis=0, tiled=True)  144 us
    ppermute x21, waiting for transfers between devices, padded(): after = lax.ppermute(leading, axis, down)  124 us
    ppermute x21, starting transfers between devices, padded(): before = lax.ppermute(last, axis, up)  123 us
    gather x17, local copies, waits for them, and re-layouts, apply_local(): picked = jnp.swapaxes(extended[:, local_cols], 0, 1)  115 us
    ppermute x21, starting transfers between devices, padded(): after = lax.ppermute(leading, axis, down)  57.4 us
    psum x2, blocking collectives, shards(): partial_sum = lax.psum(partial_sum, 'sec')  48.3 us
    transpose x17, local copies, waits for them, and re-layouts, apply_local(): picked = jnp.swapaxes(extended[:, local_cols], 0, 1)  30.7 us
    concatenate x29, local copies, waits for them, and re-layouts, padded(): array = jnp.concatenate([before, array, after], axis=dim)  25 us
  transfers between devices with their start and end apart: 46, of which 23 were waited for; matrix products, arithmetic and copies ran while one was open for 1% of the time, Pallas kernels for 0%

commit v1 on v0

--- a/solution.py
+++ b/solution.py
@@ -100,7 +100,9 @@
         coarse_res = coarse_rhs - coarse_apply(coarse_sol)
         parts = jnp.sum(section_prolong * coarse_res[None, :, None, :], axis=(1, 3))
         width = parts.shape[1]
-        every = lax.all_gather(parts[None], "slab", axis=0, tiled=True)
+        every = jnp.concatenate(
+            lax.all_to_all(jnp.stack([parts[None]] * lax.axis_size("slab")), "slab", 0, 0), axis=0
+        )
         zero = jnp.zeros((1, width), jnp.float32)
         total = (
             every[:, 1]

time: 763 us -> 615 us (0.81)
  blocking collectives: 192 us -> 92.6 us
  starting transfers between devices: 191 us -> 142 us
    all_gather x2 -> x0, blocking collectives: 144 us -> none  [shards(): every = lax.all_gather(parts[None], 'slab', axis=0, tiled=True)]
    ppermute x21, starting transfers between devices: 123 us -> 73.6 us  [padded(): before = lax.ppermute(last, axis, up)]
    all_to_all x0 -> x2, blocking collectives: none -> 44.3 us  [shards(): lax.all_to_all(jnp.stack([parts[None]] * lax.axis_size('slab')), 'slab',...]
  transfers between devices with their start and end apart: 46 -> 46, of which waited for: 23 -> 23; matrix products, arithmetic and copies ran while one was open for 1% -> 2% of each run, Pallas kernels for 0% -> 0%
where the time goes in v1:
time: 615 us; the launch traced here: 611 us
  local copies, waits for them, and re-layouts  195 us (32%)
  starting transfers between devices  142 us (23%)
  waiting for transfers between devices  131 us (21%)
  blocking collectives  92.6 us (15%)
  other arithmetic  49.8 us (8%)
    ppermute x21, waiting for transfers between devices, padded(): after = lax.ppermute(leading, axis, down)  124 us
    gather x17, local copies, waits for them, and re-layouts, apply_local(): picked = jnp.swapaxes(extended[:, local_cols], 0, 1)  115 us
    ppermute x21, starting transfers between devices, padded(): before = lax.ppermute(last, axis, up)  73.6 us
    ppermute x21, starting transfers between devices, padded(): after = lax.ppermute(leading, axis, down)  57.6 us
    psum x2, blocking collectives, shards(): partial_sum = lax.psum(partial_sum, 'sec')  48.3 us
    all_to_all x2, blocking collectives, shards(): lax.all_to_all(jnp.stack([parts[None]] * lax.axis_size('slab')), 'slab',...  44.3 us
    transpose x17, local copies, waits for them, and re-layouts, apply_local(): picked = jnp.swapaxes(extended[:, local_cols], 0, 1)  30.7 us
    concatenate x29, local copies, waits for them, and re-layouts, padded(): array = jnp.concatenate([before, array, after], axis=dim)  25 us
  transfers between devices with their start and end apart: 46, of which 23 were waited for; matrix products, arithmetic and copies ran while one was open for 2% of the time, Pallas kernels for 0%

profile of v1, /device:TPU:127, one launch (start us, length us, event | category | flops | bytes accessed | tf_op | source)
XLA Modules:
  0.0 611.1 jit_solution(4412161457592051906)
XLA Ops:
  4.9 4.9 collective-permute-start
  25.9 5.1 collective-permute-start.2
  33.6 8.1 %collective-permute-done.3 = f32[64,96]{1,0:T(8,128)S(1)} collective-permute-done((f32[64,96]{1,0:T(8,128)S(1)}, f32[64,96]{1,0:T(8,128)S(1)}, u32[]{:S(2)}, u32[]{:S(2)}) %collective-permute-start.3) | collective-permute-done | bytes 24608 | tf_op jit(solution)/shard_map/ppermute | solution.py:20
  53.9 23.9 %psum.14 = f32[6,1216]{1,0:T(8,128)S(1)} all-reduce(f32[6,1216]{1,0:T(8,128)S(1)} %copy.191), channel_id=1, replica_groups=mesh['slab'=64,'sec'=8] {'sec'}, use_global_device_ids=true, to_apply=%region_4.5 | all-reduce | flops 7296 | bytes 58368 | tf_op jit(solution)/shard_map/psum | solution.py:94
  100.5 11.9 %gather_fusion.4 = f32[3072,6]{1,0:T(8,128)} fusion(f32[6,1216]{0,1:T(8,128)} %copy.192, s32[3072]{0:T(1024)S(1)} %broadcast_clamp_fusion), kind=kCustom, calls=%fused_computation.4 | custom fusion | bytes 159744 | tf_op jit(solution)/shard_map/gather | solution.py:36
  120.8 4.3 collective-permute-done.9
  126.3 11.9 %gather_fusion.5 = f32[3072,6]{1,0:T(8,128)} fusion(f32[6,1216]{0,1:T(8,128)} %copy.194, s32[3072]{0:T(1024)S(1)} %broadcast_clamp_fusion), kind=kCustom, calls=%fused_computation.5 | custom fusion | bytes 159744 | tf_op jit(solution)/shard_map/gather | solution.py:36
  142.7 24.2 %all_to_all.10 = f32[64,1,3,24]{3,1,2,0:T(1,128)S(1)} all-to-all(f32[64,1,3,24]{3,1,2,0:T(1,128)S(1)} %stack.6), channel_id=1, replica_groups=mesh['slab'=64,'sec'=8] {'slab'}, dimensions={0} | all-to-all | bytes 36864 | tf_op jit(solution)/shard_map/all_to_all | solution.py:104
  175.5 5.7 collective-permute-done.11
  188.0 4.3 collective-permute-done.13
  193.5 11.9 %gather_fusion.6 = f32[3072,6]{1,0:T(8,128)} fusion(f32[6,1216]{0,1:T(8,128)} %copy.198, s32[3072]{0:T(1024)S(1)} %broadcast_clamp_fusion), kind=kCustom, calls=%fused_computation.6 | custom fusion | bytes 159744 | tf_op jit(solution)/shard_map/gather | solution.py:36
  214.4 4.3 collective-permute-done.15
  221.2 11.9 %gather_fusion.7 = f32[3072,6]{1,0:T(8,128)} fusion(f32[6,1216]{0,1:T(8,128)} %copy.200, s32[3072]{0:T(1024)S(1)} %broadcast_clamp_fusion), kind=kCustom, calls=%fused_computation.7 | custom fusion | bytes 159744 | tf_op jit(solution)/shard_map/gather | solution.py:36
  252.5 13.5 %collective-permute-start.18 = (f32[64,96]{1,0:T(8,128)S(1)}, f32[64,96]{1,0:T(8,128)S(1)}, u32[]{:S(2)}, u32[]{:S(2)}) collective-permute-start(f32[64,96]{1,0:T(8,128)S(1)} %get-tuple-element.83), channel_id=1, source_target_pairs={{0,1},{1,2},{2,3},{3,4},{4,5},{5,6},{6,7},{7,8},{8,9},{9,10},{10,1... | collective-permute-start | bytes 73736 | tf_op jit(solution)/shard_map/ppermute | solution.py:19
  267.9 8.7 %collective-permute-done.19 = f32[64,96]{1,0:T(8,128)S(1)} collective-permute-done((f32[64,96]{1,0:T(8,128)S(1)}, f32[64,96]{1,0:T(8,128)S(1)}, u32[]{:S(2)}, u32[]{:S(2)}) %collective-permute-start.19) | collective-permute-done | bytes 24608 | tf_op jit(solution)/shard_map/ppermute | solution.py:20
  286.3 8.2 %collective-permute-done.21 = f32[64,96]{1,0:T(8,128)S(1)} collective-permute-done((f32[64,96]{1,0:T(8,128)S(1)}, f32[64,96]{1,0:T(8,128)S(1)}, u32[]{:S(2)}, u32[]{:S(2)}) %collective-permute-start.21) | collective-permute-done | bytes 24608 | tf_op jit(solution)/shard_map/ppermute | solution.py:20
  304.3 8.2 %collective-permute-done.23 = f32[64,96]{1,0:T(8,128)S(1)} collective-permute-done((f32[64,96]{1,0:T(8,128)S(1)}, f32[64,96]{1,0:T(8,128)S(1)}, u32[]{:S(2)}, u32[]{:S(2)}) %collective-permute-start.23) | collective-permute-done | bytes 24608 | tf_op jit(solution)/shard_map/ppermute | solution.py:20
  325.2 8.2 %collective-permute-done.25 = f32[64,96]{1,0:T(8,128)S(1)} collective-permute-done((f32[64,96]{1,0:T(8,128)S(1)}, f32[64,96]{1,0:T(8,128)S(1)}, u32[]{:S(2)}, u32[]{:S(2)}) %collective-permute-start.25) | collective-permute-done | bytes 24608 | tf_op jit(solution)/shard_map/ppermute | solution.py:20
  346.2 8.2 %collective-permute-done.27 = f32[64,96]{1,0:T(8,128)S(1)} collective-permute-done((f32[64,96]{1,0:T(8,128)S(1)}, f32[64,96]{1,0:T(8,128)S(1)}, u32[]{:S(2)}, u32[]{:S(2)}) %collective-permute-start.27) | collective-permute-done | bytes 24608 | tf_op jit(solution)/shard_map/ppermute | solution.py:20
  368.7 24.5 %psum.15 = f32[6,1216]{1,0:T(8,128)S(1)} all-reduce(f32[6,1216]{1,0:T(8,128)} %copy.215), channel_id=1, replica_groups=mesh['slab'=64,'sec'=8] {'sec'}, use_global_device_ids=true, to_apply=%region_20.21 | all-reduce | flops 7296 | bytes 58368 | tf_op jit(solution)/shard_map/psum | solution.py:94
  408.5 4.3 collective-permute-done.31
  413.9 11.9 %gather_fusion.14 = f32[3072,6]{1,0:T(8,128)} fusion(f32[6,1216]{0,1:T(8,128)} %copy.216, s32[3072]{0:T(1024)S(1)} %broadcast_clamp_fusion), kind=kCustom, calls=%fused_computation.14 | custom fusion | bytes 159744 | tf_op jit(solution)/shard_map/gather | solution.py:36
  440.3 11.9 %gather_fusion.15 = f32[3072,6]{1,0:T(8,128)} fusion(f32[6,1216]{0,1:T(8,128)} %copy.218, s32[3072]{0:T(1024)S(1)} %broadcast_clamp_fusion), kind=kCustom, calls=%fused_computation.15 | custom fusion | bytes 159744 | tf_op jit(solution)/shard_map/gather | solution.py:36
  457.4 20.2 %all_to_all.11 = f32[64,1,3,24]{3,1,2,0:T(1,128)} all-to-all(f32[64,1,3,24]{3,1,2,0:T(1,128)S(1)} %stack.7), channel_id=1, replica_groups=mesh['slab'=64,'sec'=8] {'slab'}, dimensions={0} | all-to-all | bytes 36864 | tf_op jit(solution)/shard_map/all_to_all | solution.py:104
  486.3 5.7 collective-permute-done.35
  498.8 4.3 collective-permute-done.37
  504.3 11.9 %gather_fusion.16 = f32[3072,6]{1,0:T(8,128)} fusion(f32[6,1216]{0,1:T(8,128)} %copy.222, s32[3072]{0:T(1024)S(1)} %broadcast_clamp_fusion), kind=kCustom, calls=%fused_computation.16 | custom fusion | bytes 159744 | tf_op jit(solution)/shard_map/gather | solution.py:36
  532.0 11.9 %gather_fusion.17 = f32[3072,6]{1,0:T(8,128)} fusion(f32[6,1216]{0,1:T(8,128)} %copy.224, s32[3072]{0:T(1024)S(1)} %broadcast_clamp_fusion), kind=kCustom, calls=%fused_computation.17 | custom fusion | bytes 159744 | tf_op jit(solution)/shard_map/gather | solution.py:36
  552.9 4.3 collective-permute-done.41
  563.2 13.5 %collective-permute-start.42 = (f32[64,96]{1,0:T(8,128)S(1)}, f32[64,96]{1,0:T(8,128)S(1)}, u32[]{:S(2)}, u32[]{:S(2)}) collective-permute-start(f32[64,96]{1,0:T(8,128)S(1)} %get-tuple-element.63), channel_id=1, source_target_pairs={{0,1},{1,2},{2,3},{3,4},{4,5},{5,6},{6,7},{7,8},{8,9},{9,10},{10,1... | collective-permute-start | bytes 73736 | tf_op jit(solution)/shard_map/ppermute | solution.py:19
  578.6 8.7 %collective-permute-done.43 = f32[64,96]{1,0:T(8,128)S(1)} collective-permute-done((f32[64,96]{1,0:T(8,128)S(1)}, f32[64,96]{1,0:T(8,128)S(1)}, u32[]{:S(2)}, u32[]{:S(2)}) %collective-permute-start.43) | collective-permute-done | bytes 24608 | tf_op jit(solution)/shard_map/ppermute | solution.py:20
  597.0 8.2 %collective-permute-done.45 = f32[64,96]{1,0:T(8,128)S(1)} collective-permute-done((f32[64,96]{1,0:T(8,128)S(1)}, f32[64,96]{1,0:T(8,128)S(1)}, u32[]{:S(2)}, u32[]{:S(2)}) %collective-permute-start.45) | collective-permute-done | bytes 24608 | tf_op jit(solution)/shard_map/ppermute | solution.py:20
  (291 shorter events, 281.4 us)
Async XLA Ops:
  4.9 11.6 %collective-permute-start = (f32[64,96]{1,0:T(8,128)S(1)}, f32[64,96]{1,0:T(8,128)S(1)}, u32[]{:S(2)}, u32[]{:S(2)}) collective-permute-start(f32[64,96]{1,0:T(8,128)S(1)} %get-tuple-element.97), channel_id=1, source_target_pairs={{0,1},{1,2},{2,3},{3,4},{4,5},{5,6},{6,7},{7,8},{8,9},{9,10},{10,1... | collective-permute-start | bytes 73736 | tf_op jit(solution)/shard_map/ppermute | solution.py:19
  9.8 10.7 %collective-permute-start.1 = (f32[64,96]{1,0:T(8,128)S(1)}, f32[64,96]{1,0:T(8,128)S(1)}, u32[]{:S(2)}, u32[]{:S(2)}) collective-permute-start(f32[64,96]{1,0:T(8,128)S(1)} %get-tuple-element.98), channel_id=1, source_target_pairs={{1,0},{2,1},{3,2},{4,3},{5,4},{6,5},{7,6},{8,7},{9,8},{10,9},{11,1... | collective-permute-start | bytes 73736 | tf_op jit(solution)/shard_map/ppermute | solution.py:20
  25.9 7.7 %collective-permute-start.2 = (f32[64,96]{1,0:T(8,128)S(1)}, f32[64,96]{1,0:T(8,128)S(1)}, u32[]{:S(2)}, u32[]{:S(2)}) collective-permute-start(f32[64,96]{1,0:T(8,128)S(1)} %get-tuple-element.95), channel_id=1, source_target_pairs={{0,1},{1,2},{2,3},{3,4},{4,5},{5,6},{6,7},{7,8},{8,9},{9,10},{10,1... | collective-permute-start | bytes 73736 | tf_op jit(solution)/shard_map/ppermute | solution.py:19
  31.1 10.7 %collective-permute-start.3 = (f32[64,96]{1,0:T(8,128)S(1)}, f32[64,96]{1,0:T(8,128)S(1)}, u32[]{:S(2)}, u32[]{:S(2)}) collective-permute-start(f32[64,96]{1,0:T(8,128)S(1)} %get-tuple-element.96), channel_id=1, source_target_pairs={{1,0},{2,1},{3,2},{4,3},{5,4},{6,5},{7,6},{8,7},{9,8},{10,9},{11,1... | collective-permute-start | bytes 73736 | tf_op jit(solution)/shard_map/ppermute | solution.py:20
  77.8 7.3 %collective-permute-start.4 = (f32[6,96]{1,0:T(8,128)S(1)}, f32[6,96]{1,0:T(8,128)S(1)}, u32[]{:S(2)}, u32[]{:S(2)}) collective-permute-start(f32[6,96]{1,0:T(8,128)S(1)} %get-tuple-element.56), channel_id=1, source_target_pairs={{0,8},{8,16},{16,24},{24,32},{32,40},{40,48},{48,56},{56,64},{64,7... | collective-permute-start | bytes 6920 | tf_op jit(solution)/shard_map/ppermute | solution.py:28
  81.8 7.7 %collective-permute-start.5 = (f32[6,96]{1,0:T(8,128)S(1)}, f32[6,96]{1,0:T(8,128)S(1)}, u32[]{:S(2)}, u32[]{:S(2)}) collective-permute-start(f32[6,96]{1,0:T(8,128)S(1)} %get-tuple-element.55), channel_id=1, source_target_pairs={{8,0},{16,8},{24,16},{32,24},{40,32},{48,40},{56,48},{64,56},{72,6... | collective-permute-start | bytes 6920 | tf_op jit(solution)/shard_map/ppermute | solution.py:28
  89.8 6.0 collective-permute-start.6
  91.7 7.7 %collective-permute-start.7 = (f32[6,96]{1,0:T(8,128)S(1)}, f32[6,96]{1,0:T(8,128)S(1)}, u32[]{:S(2)}, u32[]{:S(2)}) collective-permute-start(f32[6,96]{1,0:T(8,128)S(1)} %get-tuple-element.93), channel_id=1, source_target_pairs={{8,0},{16,8},{24,16},{32,24},{40,32},{48,40},{56,48},{64,56},{72,6... | collective-permute-start | bytes 6920 | tf_op jit(solution)/shard_map/ppermute | solution.py:20
  117.4 7.7 %collective-permute-start.9 = (f32[6,96]{1,0:T(8,128)S(1)}, f32[6,96]{1,0:T(8,128)S(1)}, u32[]{:S(2)}, u32[]{:S(2)}) collective-permute-start(f32[6,96]{1,0:T(8,128)S(1)} %get-tuple-element.91), channel_id=1, source_target_pairs={{8,0},{16,8},{24,16},{32,24},{40,32},{48,40},{56,48},{64,56},{72,6... | collective-permute-start | bytes 6920 | tf_op jit(solution)/shard_map/ppermute | solution.py:20
  169.5 6.0 collective-permute-start.10
  173.5 7.6 %collective-permute-start.11 = (f32[1,24]{1,0:T(1,128)S(1)}, f32[1,24]{1,0:T(1,128)S(1)}, u32[]{:S(2)}, u32[]{:S(2)}) collective-permute-start(f32[1,24]{1,0:T(1,128)S(1)} %fusion.65), channel_id=1, source_target_pairs={{8,0},{16,8},{24,16},{32,24},{40,32},{48,40},{56,48},{64,56},{72,6... | collective-permute-start | bytes 296 | tf_op jit(solution)/shard_map/ppermute | solution.py:20
  184.6 7.7 %collective-permute-start.13 = (f32[6,96]{1,0:T(8,128)S(1)}, f32[6,96]{1,0:T(8,128)S(1)}, u32[]{:S(2)}, u32[]{:S(2)}) collective-permute-start(f32[6,96]{1,0:T(8,128)S(1)} %get-tuple-element.89), channel_id=1, source_target_pairs={{8,0},{16,8},{24,16},{32,24},{40,32},{48,40},{56,48},{64,56},{72,6... | collective-permute-start | bytes 6920 | tf_op jit(solution)/shard_map/ppermute | solution.py:20
  211.0 7.7 %collective-permute-start.15 = (f32[6,96]{1,0:T(8,128)S(1)}, f32[6,96]{1,0:T(8,128)S(1)}, u32[]{:S(2)}, u32[]{:S(2)}) collective-permute-start(f32[6,96]{1,0:T(8,128)S(1)} %get-tuple-element.87), channel_id=1, source_target_pairs={{8,0},{16,8},{24,16},{32,24},{40,32},{48,40},{56,48},{64,56},{72,6... | collective-permute-start | bytes 6920 | tf_op jit(solution)/shard_map/ppermute | solution.py:20
  238.8 7.7 %collective-permute-start.17 = (f32[6,96]{1,0:T(8,128)S(1)}, f32[6,96]{1,0:T(8,128)S(1)}, u32[]{:S(2)}, u32[]{:S(2)}) collective-permute-start(f32[6,96]{1,0:T(8,128)S(1)} %get-tuple-element.85), channel_id=1, source_target_pairs={{8,0},{16,8},{24,16},{32,24},{40,32},{48,40},{56,48},{64,56},{72,6... | collective-permute-start | bytes 6920 | tf_op jit(solution)/shard_map/ppermute | solution.py:20
  252.5 15.4 %collective-permute-start.18 = (f32[64,96]{1,0:T(8,128)S(1)}, f32[64,96]{1,0:T(8,128)S(1)}, u32[]{:S(2)}, u32[]{:S(2)}) collective-permute-start(f32[64,96]{1,0:T(8,128)S(1)} %get-tuple-element.83), channel_id=1, source_target_pairs={{0,1},{1,2},{2,3},{3,4},{4,5},{5,6},{6,7},{7,8},{8,9},{9,10},{10,1... | collective-permute-start | bytes 73736 | tf_op jit(solution)/shard_map/ppermute | solution.py:19
  265.9 10.7 %collective-permute-start.19 = (f32[64,96]{1,0:T(8,128)S(1)}, f32[64,96]{1,0:T(8,128)S(1)}, u32[]{:S(2)}, u32[]{:S(2)}) collective-permute-start(f32[64,96]{1,0:T(8,128)S(1)} %get-tuple-element.84), channel_id=1, source_target_pairs={{1,0},{2,1},{3,2},{4,3},{5,4},{6,5},{7,6},{8,7},{9,8},{10,9},{11,1... | collective-permute-start | bytes 73736 | tf_op jit(solution)/shard_map/ppermute | solution.py:20
  283.9 10.7 %collective-permute-start.21 = (f32[64,96]{1,0:T(8,128)S(1)}, f32[64,96]{1,0:T(8,128)S(1)}, u32[]{:S(2)}, u32[]{:S(2)}) collective-permute-start(f32[64,96]{1,0:T(8,128)S(1)} %get-tuple-element.82), channel_id=1, source_target_pairs={{1,0},{2,1},{3,2},{4,3},{5,4},{6,5},{7,6},{8,7},{9,8},{10,9},{11,1... | collective-permute-start | bytes 73736 | tf_op jit(solution)/shard_map/ppermute | solution.py:20
  301.8 10.7 %collective-permute-start.23 = (f32[64,96]{1,0:T(8,128)S(1)}, f32[64,96]{1,0:T(8,128)S(1)}, u32[]{:S(2)}, u32[]{:S(2)}) collective-permute-start(f32[64,96]{1,0:T(8,128)S(1)} %get-tuple-element.80), channel_id=1, source_target_pairs={{1,0},{2,1},{3,2},{4,3},{5,4},{6,5},{7,6},{8,7},{9,8},{10,9},{11,1... | collective-permute-start | bytes 73736 | tf_op jit(solution)/shard_map/ppermute | solution.py:20
  322.8 10.7 %collective-permute-start.25 = (f32[64,96]{1,0:T(8,128)S(1)}, f32[64,96]{1,0:T(8,128)S(1)}, u32[]{:S(2)}, u32[]{:S(2)}) collective-permute-start(f32[64,96]{1,0:T(8,128)S(1)} %get-tuple-element.78), channel_id=1, source_target_pairs={{1,0},{2,1},{3,2},{4,3},{5,4},{6,5},{7,6},{8,7},{9,8},{10,9},{11,1... | collective-permute-start | bytes 73736 | tf_op jit(solution)/shard_map/ppermute | solution.py:20
  343.8 10.7 %collective-permute-start.27 = (f32[64,96]{1,0:T(8,128)S(1)}, f32[64,96]{1,0:T(8,128)S(1)}, u32[]{:S(2)}, u32[]{:S(2)}) collective-permute-start(f32[64,96]{1,0:T(8,128)S(1)} %get-tuple-element.76), channel_id=1, source_target_pairs={{1,0},{2,1},{3,2},{4,3},{5,4},{6,5},{7,6},{8,7},{9,8},{10,9},{11,1... | collective-permute-start | bytes 73736 | tf_op jit(solution)/shard_map/ppermute | solution.py:20
  395.2 7.7 %collective-permute-start.29 = (f32[6,96]{1,0:T(8,128)S(1)}, f32[6,96]{1,0:T(8,128)S(1)}, u32[]{:S(2)}, u32[]{:S(2)}) collective-permute-start(f32[6,96]{1,0:T(8,128)S(1)} %get-tuple-element.53), channel_id=1, source_target_pairs={{8,0},{16,8},{24,16},{32,24},{40,32},{48,40},{56,48},{64,56},{72,6... | collective-permute-start | bytes 6920 | tf_op jit(solution)/shard_map/ppermute | solution.py:28
  405.1 7.7 %collective-permute-start.31 = (f32[6,96]{1,0:T(8,128)S(1)}, f32[6,96]{1,0:T(8,128)S(1)}, u32[]{:S(2)}, u32[]{:S(2)}) collective-permute-start(f32[6,96]{1,0:T(8,128)S(1)} %get-tuple-element.73), channel_id=1, source_target_pairs={{8,0},{16,8},{24,16},{32,24},{40,32},{48,40},{56,48},{64,56},{72,6... | collective-permute-start | bytes 6920 | tf_op jit(solution)/shard_map/ppermute | solution.py:20
  429.6 5.5 collective-permute-start.32
  431.5 7.7 %collective-permute-start.33 = (f32[6,96]{1,0:T(8,128)S(1)}, f32[6,96]{1,0:T(8,128)S(1)}, u32[]{:S(2)}, u32[]{:S(2)}) collective-permute-start(f32[6,96]{1,0:T(8,128)S(1)} %get-tuple-element.71), channel_id=1, source_target_pairs={{8,0},{16,8},{24,16},{32,24},{40,32},{48,40},{56,48},{64,56},{72,6... | collective-permute-start | bytes 6920 | tf_op jit(solution)/shard_map/ppermute | solution.py:20
  480.3 6.0 collective-permute-start.34
  484.4 7.6 %collective-permute-start.35 = (f32[1,24]{1,0:T(1,128)S(1)}, f32[1,24]{1,0:T(1,128)S(1)}, u32[]{:S(2)}, u32[]{:S(2)}) collective-permute-start(f32[1,24]{1,0:T(1,128)S(1)} %fusion.66), channel_id=1, source_target_pairs={{8,0},{16,8},{24,16},{32,24},{40,32},{48,40},{56,48},{64,56},{72,6... | collective-permute-start | bytes 296 | tf_op jit(solution)/shard_map/ppermute | solution.py:20
  495.4 7.7 %collective-permute-start.37 = (f32[6,96]{1,0:T(8,128)S(1)}, f32[6,96]{1,0:T(8,128)S(1)}, u32[]{:S(2)}, u32[]{:S(2)}) collective-permute-start(f32[6,96]{1,0:T(8,128)S(1)} %get-tuple-element.69), channel_id=1, source_target_pairs={{8,0},{16,8},{24,16},{32,24},{40,32},{48,40},{56,48},{64,56},{72,6... | collective-permute-start | bytes 6920 | tf_op jit(solution)/shard_map/ppermute | solution.py:20
  521.8 7.7 %collective-permute-start.39 = (f32[6,96]{1,0:T(8,128)S(1)}, f32[6,96]{1,0:T(8,128)S(1)}, u32[]{:S(2)}, u32[]{:S(2)}) collective-permute-start(f32[6,96]{1,0:T(8,128)S(1)} %get-tuple-element.67), channel_id=1, source_target_pairs={{8,0},{16,8},{24,16},{32,24},{40,32},{48,40},{56,48},{64,56},{72,6... | collective-permute-start | bytes 6920 | tf_op jit(solution)/shard_map/ppermute | solution.py:20
  549.6 7.7 %collective-permute-start.41 = (f32[6,96]{1,0:T(8,128)S(1)}, f32[6,96]{1,0:T(8,128)S(1)}, u32[]{:S(2)}, u32[]{:S(2)}) collective-permute-start(f32[6,96]{1,0:T(8,128)S(1)} %get-tuple-element.65), channel_id=1, source_target_pairs={{8,0},{16,8},{24,16},{32,24},{40,32},{48,40},{56,48},{64,56},{72,6... | collective-permute-start | bytes 6920 | tf_op jit(solution)/shard_map/ppermute | solution.py:20
  563.2 15.4 %collective-permute-start.42 = (f32[64,96]{1,0:T(8,128)S(1)}, f32[64,96]{1,0:T(8,128)S(1)}, u32[]{:S(2)}, u32[]{:S(2)}) collective-permute-start(f32[64,96]{1,0:T(8,128)S(1)} %get-tuple-element.63), channel_id=1, source_target_pairs={{0,1},{1,2},{2,3},{3,4},{4,5},{5,6},{6,7},{7,8},{8,9},{9,10},{10,1... | collective-permute-start | bytes 73736 | tf_op jit(solution)/shard_map/ppermute | solution.py:19
  576.7 10.7 %collective-permute-start.43 = (f32[64,96]{1,0:T(8,128)S(1)}, f32[64,96]{1,0:T(8,128)S(1)}, u32[]{:S(2)}, u32[]{:S(2)}) collective-permute-start(f32[64,96]{1,0:T(8,128)S(1)} %get-tuple-element.64), channel_id=1, source_target_pairs={{1,0},{2,1},{3,2},{4,3},{5,4},{6,5},{7,6},{8,7},{9,8},{10,9},{11,1... | collective-permute-start | bytes 73736 | tf_op jit(solution)/shard_map/ppermute | solution.py:20
  594.6 10.7 %collective-permute-start.45 = (f32[64,96]{1,0:T(8,128)S(1)}, f32[64,96]{1,0:T(8,128)S(1)}, u32[]{:S(2)}, u32[]{:S(2)}) collective-permute-start(f32[64,96]{1,0:T(8,128)S(1)} %get-tuple-element.62), channel_id=1, source_target_pairs={{1,0},{2,1},{3,2},{4,3},{5,4},{6,5},{7,6},{8,7},{9,8},{10,9},{11,1... | collective-permute-start | bytes 73736 | tf_op jit(solution)/shard_map/ppermute | solution.py:20
  (31 other events, 540.6 us)
